TPU v7x, 32 devices: a whole 2x2x4 slice. The times are simulated.
32 devices in a mesh: energy: 8 (over z, y), slab: 4 (over x, core).
Axes of the slice: x: 2, y: 2, z: 4, core: 2. Of those that a mesh axis runs over, the one named last changes fastest.
Arguments:
- green: bfloat16 [8, 4, 2, 512, 512], P('energy', 'slab'), may hold values from -3 to 3
- sigma: bfloat16 [8, 4, 2, 512, 512], P('energy', 'slab'), may hold values from -0.035888672 to 0.035888672
- tiles: int32 [4, 16], P('slab'), may hold values from 0 to 511, as said below
- owner: int32 [4, 16], P('slab'), may hold values from 0 to 7, as said below
- energy_order: int32 [8], replicated, may hold values from 0 to 7, each once
Outputs:
- polar: bfloat16 [4, 32, 2, 8, 1, 512], P('slab', 'energy')
Inputs may be any that keep to these rules, and one draw needn't show every extreme that they name: The tiles of one slab are distinct. No owner holds more than 4 tiles of one slab; in every slab some owner holds exactly 4.
All inputs are finite; a program needn't handle non-finite values.
Results may differ from a plain program's by a relative error of at most 0.008.
Values may be sent and summed in bfloat16 or wider, within the bound.
A program may use at most 64 MiB of HBM per device.

v0:
```python
import math

import jax
import jax.numpy as jnp
from jax import lax
from jax.sharding import PartitionSpec as P

STRIP = 1
CAP = 4


def padded(array, sides, width):
    for axis, dim in sides:
        peers, length = (lax.axis_size(axis), array.shape[dim])
        up = [(i, (i + 1) % peers) for i in range(peers - 1)]
        down = [(j, i) for i, j in up]
        last = lax.slice_in_dim(array, length - width, length, axis=dim)
        first = lax.slice_in_dim(array, 0, width, axis=dim)
        before = lax.ppermute(last, axis, up)
        after = lax.ppermute(first, axis, down)
        array = jnp.concatenate([before, array, after], axis=dim)
    return array


def times_adjoint(left, right):
    return lax.dot_general(
        left, right, (((1,), (1,)), ((), ())), preferred_element_type=jnp.float32
    )


def split_table(table):
    upper = table.astype(jnp.bfloat16)
    lower = (table - upper.astype(jnp.float32)).astype(jnp.bfloat16)
    return (upper, lower)


def on_device(green, sigma, tiles, owner, energy_order):
    strip = STRIP
    block = green.shape[-1]
    listed = tiles.shape[1]
    count = lax.axis_size("energy")
    nfft = 2 * count
    capacity = CAP
    beside_all = padded(sigma, (("slab", 1),), 1)
    eff = (
        beside_all[0, 0].astype(jnp.float32)
        + beside_all[0, 1].astype(jnp.float32)
        + beside_all[0, 2].astype(jnp.float32)
    ).astype(jnp.bfloat16)
    g_re, g_im = (green[0, 0, 0], green[0, 0, 1])
    s_re, s_im = (eff[0], eff[1])
    p_re = (
        jnp.dot(g_re, s_re, preferred_element_type=jnp.float32)
        - jnp.dot(g_im, s_im, preferred_element_type=jnp.float32)
    ).astype(jnp.bfloat16)
    p_im = (
        jnp.dot(g_re, s_im, preferred_element_type=jnp.float32)
        + jnp.dot(g_im, s_re, preferred_element_type=jnp.float32)
    ).astype(jnp.bfloat16)
    row_index = (tiles[0][:, None] * strip + jnp.arange(strip, dtype=jnp.int32)[None, :]).reshape(
        -1
    )
    full_re = times_adjoint(p_re, g_re) + times_adjoint(p_im, g_im)
    full_im = times_adjoint(p_im, g_re) - times_adjoint(p_re, g_im)
    l_re = full_re[row_index]
    l_im = full_im[row_index]
    d_re = g_re[row_index].astype(jnp.float32) - g_re[:, row_index].T.astype(jnp.float32)
    d_im = g_im[row_index].astype(jnp.float32) + g_im[:, row_index].T.astype(jnp.float32)
    planes = jnp.stack(
        [
            l_re.astype(jnp.bfloat16),
            l_im.astype(jnp.bfloat16),
            (l_re + d_re).astype(jnp.bfloat16),
            (l_im + d_im).astype(jnp.bfloat16),
        ]
    )
    planes = planes.transpose(1, 0, 2).reshape(listed, 4 * strip * block)
    own = owner[0]
    position = jnp.arange(listed, dtype=jnp.int32)
    earlier = (own[:, None] == own[None, :]) & (position[:, None] < position[None, :])
    rank = jnp.sum(earlier.astype(jnp.int32), axis=0)
    slot = own * capacity + rank
    selector = (jnp.arange(count * capacity, dtype=jnp.int32)[:, None] == slot[None, :]).astype(
        jnp.bfloat16
    )
    outgoing = jnp.dot(selector, planes, preferred_element_type=jnp.float32).astype(jnp.bfloat16)
    outgoing = outgoing.reshape(count, capacity, 4, strip, block)
    freq = jnp.arange(nfft, dtype=jnp.int32)
    phase_fwd = (freq[:, None] * energy_order[None, :] % nfft).astype(jnp.float32) * (
        2.0 * math.pi / nfft
    )
    cos_hi, cos_lo = split_table(jnp.cos(phase_fwd))
    sin_hi, sin_lo = split_table(jnp.sin(phase_fwd))
    forward_table = jnp.concatenate(
        [jnp.concatenate([cos_hi, cos_lo], axis=1), jnp.concatenate([sin_hi, sin_lo], axis=1)],
        axis=0,
    )
    lags = jnp.arange(count, dtype=jnp.int32)
    phase_inv = (lags[:, None] * freq[None, :] % nfft).astype(jnp.float32) * (2.0 * math.pi / nfft)
    cos_inv, sin_inv = (jnp.cos(phase_inv), jnp.sin(phase_inv))
    inverse_table = jnp.concatenate(
        [jnp.concatenate([cos_inv, -sin_inv], axis=1), jnp.concatenate([sin_inv, cos_inv], axis=1)],
        axis=0,
    )
    scale = 1.0 / (nfft * count)
    items = lax.all_to_all(outgoing, "energy", split_axis=0, concat_axis=0, tiled=True)
    items_count = items.shape[1]
    flat = items.reshape(items.shape[0], -1)
    doubled = jnp.concatenate([flat, flat], axis=0)
    spectra = jnp.dot(forward_table, doubled, preferred_element_type=jnp.float32)
    spectra = spectra.reshape(2, nfft, items_count, 4, strip, block)
    with_cos = spectra[0]
    with_sin = spectra[1]
    less_re = with_cos[:, :, 0] + with_sin[:, :, 1]
    less_im = with_cos[:, :, 1] - with_sin[:, :, 0]
    great_re = with_cos[:, :, 2] + with_sin[:, :, 3]
    great_im = with_cos[:, :, 3] - with_sin[:, :, 2]
    prod_re = less_re * great_re + less_im * great_im
    prod_im = less_im * great_re - less_re * great_im
    stacked = jnp.concatenate([prod_re, prod_im], axis=0).reshape(2 * nfft, -1)
    lagged = jnp.dot(
        inverse_table, stacked, precision=lax.Precision.HIGH, preferred_element_type=jnp.float32
    )
    lagged = lagged.reshape(2, count, items_count, strip, block).transpose(2, 0, 1, 3, 4)
    result = (lagged * scale).astype(jnp.bfloat16)
    return result.reshape(1, capacity, 2, count, strip, block)


def solution(mesh):
    placed = (
        P("energy", "slab", None, None, None),
        P("energy", "slab", None, None, None),
        P("slab", None),
        P("slab", None),
        P(),
    )
    return jax.shard_map(
        on_device,
        mesh=mesh,
        in_specs=placed,
        out_specs=P("slab", "energy", None, None, None, None),
        check_vma=False,
    )
```

profile of v0, /device:TPU:1, one launch (start us, length us, event | category | flops | bytes accessed | tf_op | source)
XLA Modules:
  0.0 48.8 jit_solution(2502344618542921053)
XLA Ops:
  0.0 4.5 %collective-permute-start = (bf16[1,1,2,512,512]{4,3,2,1,0:T(8,128)(2,1)}, bf16[1,1,2,512,512]{4,3,2,1,0:T(8,128)(2,1)}, u32[]{:S(2)}, u32[]{:S(2)}) collective-permute-start(bf16[1,1,2,512,512]{4,3,2,1,0:T(8,128)(2,1)} %param.6), channel_id=1, source_target_pairs={{0,1},{1,2},{2,3},{4,5},{5,6},{6,7},{8,9},{9,10},{10,11},{12,13},{... | collective-permute-start | bytes 3145736 | tf_op jit(solution)/shard_map/ppermute | solution.py:19
  4.5 1.9 %collective-permute-start.1 = (bf16[1,1,2,512,512]{4,3,2,1,0:T(8,128)(2,1)}, bf16[1,1,2,512,512]{4,3,2,1,0:T(8,128)(2,1)}, u32[]{:S(2)}, u32[]{:S(2)}) collective-permute-start(bf16[1,1,2,512,512]{4,3,2,1,0:T(8,128)(2,1)} %param.6), channel_id=1, source_target_pairs={{1,0},{2,1},{3,2},{5,4},{6,5},{7,6},{9,8},{10,9},{11,10},{13,12},{... | collective-permute-start | bytes 3145736 | tf_op jit(solution)/shard_map/ppermute | solution.py:20
  6.4 1.3 %slice_bitcast_fusion.3 = (bf16[512,512]{1,0:T(8,128)(2,1)S(1)}, bf16[512,512]{1,0:T(8,128)(2,1)S(1)}) fusion(bf16[1,1,2,512,512]{4,3,2,1,0:T(8,128)(2,1)} %param.5), kind=kLoop, calls=%fused_computation.20 | loop fusion | bytes 2097152 | tf_op jit(solution)/shard_map/squeeze | solution.py:50
  7.7 0.0 copy-start.3
  7.7 0.2 copy.26
  7.9 0.2 copy.27
  8.1 0.2 copy-done.3
  8.4 0.6 %gather_fusion.2 = bf16[16,512]{1,0:T(8,128)(2,1)S(1)} fusion(bf16[512,512]{1,0:T(8,128)(2,1)S(1)} %get-tuple-element.9, s32[1024]{0:T(1024)S(1)} %pad_clamp_fusion), kind=kCustom, calls=%fused_computation.2 | custom fusion | bytes 32832 | tf_op jit(solution)/shard_map/gather | solution.py:67
  9.0 0.6 %gather_fusion.4 = bf16[16,512]{1,0:T(8,128)(2,1)S(1)} fusion(bf16[512,512]{1,0:T(8,128)(2,1)S(1)} %get-tuple-element.10, s32[1024]{0:T(1024)S(1)} %pad_clamp_fusion), kind=kCustom, calls=%fused_computation.4 | custom fusion | bytes 32832 | tf_op jit(solution)/shard_map/gather | solution.py:68
  9.6 0.0 copy-start.4
  9.6 0.0 copy-start.1
  9.6 0.6 %gather_fusion.3 = bf16[16,512]{1,0:T(8,128)(2,1)S(1)} fusion(bf16[512,512]{0,1:T(8,128)(2,1)S(1)} %copy.26, s32[1024]{0:T(1024)S(1)} %pad_clamp_fusion), kind=kCustom, calls=%fused_computation.3 | custom fusion | bytes 32832 | tf_op jit(solution)/shard_map/gather | solution.py:67
  10.2 0.6 %gather_fusion.5 = bf16[16,512]{1,0:T(8,128)(2,1)S(1)} fusion(bf16[512,512]{0,1:T(8,128)(2,1)S(1)} %copy.27, s32[1024]{0:T(1024)S(1)} %pad_clamp_fusion), kind=kCustom, calls=%fused_computation.5 | custom fusion | bytes 32832 | tf_op jit(solution)/shard_map/gather | solution.py:68
  10.8 0.1 fusion.48
  10.8 0.0 copy-done.4
  10.8 0.1 convert_reduce_fusion
  10.9 0.0 copy-start
  10.9 5.6 %collective-permute-done = bf16[1,1,2,512,512]{4,3,2,1,0:T(8,128)(2,1)} collective-permute-done((bf16[1,1,2,512,512]{4,3,2,1,0:T(8,128)(2,1)}, bf16[1,1,2,512,512]{4,3,2,1,0:T(8,128)(2,1)}, u32[]{:S(2)}, u32[]{:S(2)}) %collective-permute-start) | collective-permute-done | bytes 1048608 | tf_op jit(solution)/shard_map/ppermute | solution.py:19
  16.5 4.4 %collective-permute-done.1 = bf16[1,1,2,512,512]{4,3,2,1,0:T(8,128)(2,1)} collective-permute-done((bf16[1,1,2,512,512]{4,3,2,1,0:T(8,128)(2,1)}, bf16[1,1,2,512,512]{4,3,2,1,0:T(8,128)(2,1)}, u32[]{:S(2)}, u32[]{:S(2)}) %collective-permute-start.1) | collective-permute-done | bytes 1048608 | tf_op jit(solution)/shard_map/ppermute | solution.py:20
  20.9 0.0 copy-done.1
  20.9 2.0 %add_convert_fusion = bf16[1,1,2,512,512]{4,3,2,1,0:T(8,128)(2,1)S(1)} fusion(bf16[1,1,2,512,512]{4,3,2,1,0:T(8,128)(2,1)} %collective-permute-done.1, bf16[1,1,2,512,512]{4,3,2,1,0:T(8,128)(2,1)S(1)} %copy-done.1, bf16[1,1,2,512,512]{4,3,2,1,0:T(8,128)(2,1)} %collective-permute-done), kind=kLoop, calls=%fused_computation.7 | loop fusion | flops 3145728 | bytes 4194304 | tf_op jit(solution)/shard_map/convert_element_type | solution.py:49
  22.9 0.0 copy-done
  22.9 0.5 fusion.5
  23.4 0.5 fusion.4
  23.9 0.5 fusion
  24.4 0.5 fusion.56
  24.9 0.5 fusion.1
  25.4 0.5 fusion.55
  25.9 1.5 %convolution_add_fusion = f32[512,512]{1,0:T(8,128)} fusion(f32[512,512]{1,0:T(8,128)S(1)} %fusion.56, bf16[512,512]{1,0:T(8,128)(2,1)S(1)} %fusion.1, bf16[1,1,2,512,512]{4,3,2,1,0:T(8,128)(2,1)S(1)} %copy-done), kind=kOutput, calls=%fused_computation.9 | convolution fusion | flops 268697600 | bytes 3145728 | tf_op jit(solution)/shard_map/dot_general | solution.py:26
  27.3 1.8 %gather_fusion = f32[16,512]{1,0:T(8,128)S(1)} fusion(f32[512,512]{1,0:T(8,128)} %convolution_add_fusion, s32[1024]{0:T(1024)S(1)} %pad_clamp_fusion), kind=kCustom, calls=%fused_computation | custom fusion | bytes 65600 | tf_op jit(solution)/shard_map/gather | solution.py:65
  29.1 1.5 %convolution_subtract_fusion = f32[512,512]{1,0:T(8,128)} fusion(f32[512,512]{1,0:T(8,128)S(1)} %fusion.55, bf16[512,512]{1,0:T(8,128)(2,1)S(1)} %fusion, bf16[1,1,2,512,512]{4,3,2,1,0:T(8,128)(2,1)S(1)} %copy-done), kind=kOutput, calls=%fused_computation.8 | convolution fusion | flops 268697600 | bytes 3145728 | tf_op jit(solution)/shard_map/dot_general | solution.py:26
  30.6 0.0 copy-start.2
  30.6 1.8 %gather_fusion.1 = f32[16,512]{1,0:T(8,128)S(1)} fusion(f32[512,512]{1,0:T(8,128)} %convolution_subtract_fusion, s32[1024]{0:T(1024)S(1)} %pad_clamp_fusion), kind=kCustom, calls=%fused_computation.1 | custom fusion | bytes 65600 | tf_op jit(solution)/shard_map/gather | solution.py:66
  32.5 0.2 convolution_convert_fusion
  32.7 0.7 %reshape.149 = bf16[8,4,4,1,512]{4,2,1,0,3:T(4,128)(2,1)} reshape(bf16[32,2048]{1,0:T(8,128)(2,1)S(1)} %convolution_convert_fusion) | data formatting | bytes 262144 | tf_op jit(solution)/shard_map/reshape | solution.py:87
  33.4 5.6 %all-to-all-start = ((bf16[8,4,4,1,512]{4,2,1,3,0:T(4,128)(2,1)}), bf16[8,4,4,1,512]{4,2,1,3,0:T(4,128)(2,1)S(1)}, u32[]{:S(2)}, u32[]{:S(2)}) async-start(bf16[8,4,4,1,512]{4,2,1,3,0:T(4,128)(2,1)} %bitcast.17), calls=%async_computation | async-start | bytes 262144 | tf_op jit(solution)/shard_map/all_to_all | solution.py:106
  38.9 0.1 fusion.50
  39.0 0.0 copy-done.2
  39.0 0.1 fusion.46
  39.1 6.0 %all-to-all-done = bf16[8,4,4,1,512]{4,2,1,3,0:T(4,128)(2,1)S(1)} async-done(((bf16[8,4,4,1,512]{4,2,1,3,0:T(4,128)(2,1)}), bf16[8,4,4,1,512]{4,2,1,3,0:T(4,128)(2,1)S(1)}, u32[]{:S(2)}, u32[]{:S(2)}) %all-to-all-start) | async-done | bytes 131104 | tf_op jit(solution)/shard_map/all_to_all | solution.py:106
  45.1 0.1 reshape.150
  45.2 0.4 fusion.7
  45.6 0.1 fusion.57
  45.7 0.4 squeeze.16
  46.0 0.4 squeeze.17
  46.4 1.4 %add_reduce_fusion = (f32[16,4,512]{2,1,0:T(4,128)S(1)}, f32[16,4,512]{2,1,0:T(4,128)S(1)}) fusion(f32[16,4,4,1,512]{4,2,1,0,3:T(4,128)S(1)} %squeeze.17, f32[16,4,4,1,512]{4,2,1,0,3:T(4,128)S(1)} %squeeze.16), kind=kLoop, calls=%fused_computation.35 | loop fusion | flops 327680 | bytes 1310720 | tf_op jit(solution)/shard_map/add | solution.py:118
  47.9 0.3 fusion.3
  48.1 0.6 %copy.31 = bf16[1,4,2,8,1,512]{5,3,4,2,1,0:T(8,128)(2,1)} copy(bf16[1,4,2,8,1,512]{5,3,1,2,4,0:T(8,128)(2,1)S(1)} %fusion.3) | data formatting | bytes 131072 | tf_op jit(solution)/shard_map/reshape | solution.py:126
  (9 shorter events, 0.2 us)
Async XLA Ops:
  0.0 16.5 %collective-permute-start = (bf16[1,1,2,512,512]{4,3,2,1,0:T(8,128)(2,1)}, bf16[1,1,2,512,512]{4,3,2,1,0:T(8,128)(2,1)}, u32[]{:S(2)}, u32[]{:S(2)}) collective-permute-start(bf16[1,1,2,512,512]{4,3,2,1,0:T(8,128)(2,1)} %param.6), channel_id=1, source_target_pairs={{0,1},{1,2},{2,3},{4,5},{5,6},{6,7},{8,9},{9,10},{10,11},{12,13},{... | collective-permute-start | bytes 3145736 | tf_op jit(solution)/shard_map/ppermute | solution.py:19
  4.5 16.4 %collective-permute-start.1 = (bf16[1,1,2,512,512]{4,3,2,1,0:T(8,128)(2,1)}, bf16[1,1,2,512,512]{4,3,2,1,0:T(8,128)(2,1)}, u32[]{:S(2)}, u32[]{:S(2)}) collective-permute-start(bf16[1,1,2,512,512]{4,3,2,1,0:T(8,128)(2,1)} %param.6), channel_id=1, source_target_pairs={{1,0},{2,1},{3,2},{5,4},{6,5},{7,6},{9,8},{10,9},{11,10},{13,12},{... | collective-permute-start | bytes 3145736 | tf_op jit(solution)/shard_map/ppermute | solution.py:20
  7.7 0.7 %copy-start.3 = (s32[1,16]{1,0:T(1,128)S(1)}, s32[1,16]{1,0:T(1,128)}, u32[]{:S(2)}) copy-start(s32[1,16]{1,0:T(1,128)} %param.7) | copy-start | bytes 196
  9.6 1.3 %copy-start.4 = (s32[1,16]{1,0:T(1,128)S(1)}, s32[1,16]{1,0:T(1,128)}, u32[]{:S(2)}) copy-start(s32[1,16]{1,0:T(1,128)} %param.8) | copy-start | bytes 196
  9.6 11.4 %copy-start.1 = (bf16[1,1,2,512,512]{4,3,2,1,0:T(8,128)(2,1)S(1)}, bf16[1,1,2,512,512]{4,3,2,1,0:T(8,128)(2,1)}, u32[]{:S(2)}) copy-start(bf16[1,1,2,512,512]{4,3,2,1,0:T(8,128)(2,1)} %param.6) | copy-start | bytes 3145732
  10.9 12.0 %copy-start = (bf16[1,1,2,512,512]{4,3,2,1,0:T(8,128)(2,1)S(1)}, bf16[1,1,2,512,512]{4,3,2,1,0:T(8,128)(2,1)}, u32[]{:S(2)}) copy-start(bf16[1,1,2,512,512]{4,3,2,1,0:T(8,128)(2,1)} %param.5) | copy-start | bytes 3145732
  30.6 8.4 %copy-start.2 = (s32[8]{0:T(128)S(1)}, s32[8]{0:T(128)}, u32[]{:S(2)}) copy-start(s32[8]{0:T(128)} %param.9) | copy-start | bytes 100
  33.4 11.8 %all-to-all-start = ((bf16[8,4,4,1,512]{4,2,1,3,0:T(4,128)(2,1)}), bf16[8,4,4,1,512]{4,2,1,3,0:T(4,128)(2,1)S(1)}, u32[]{:S(2)}, u32[]{:S(2)}) async-start(bf16[8,4,4,1,512]{4,2,1,3,0:T(4,128)(2,1)} %bitcast.17), calls=%async_computation | async-start | bytes 262144 | tf_op jit(solution)/shard_map/all_to_all | solution.py:106
where the time goes:
time: 49.1 us; the launch traced here: 48.8 us
  waiting for transfers between devices  16 us (33%)
  starting transfers between devices  12 us (24%)
  local copies, waits for them, and re-layouts  10.2 us (21%)
  matrix products  6.63 us (14%)
  other arithmetic  3.7 us (8%)
    all_to_all x1, waiting for transfers between devices, on_device(): lax.all_to_all(outgoing, 'energy', split_axis=0, concat_axis=0, tiled=True)  6.01 us
    ppermute x1, waiting for transfers between devices, padded(): before = lax.ppermute(last, axis, up)  5.6 us
    all_to_all x1, starting transfers between devices, on_device(): lax.all_to_all(outgoing, 'energy', split_axis=0, concat_axis=0, tiled=True)  5.56 us
    ppermute x1, starting transfers between devices, padded(): before = lax.ppermute(last, axis, up)  4.49 us
    ppermute x1, waiting for transfers between devices, padded(): after = lax.ppermute(first, axis, down)  4.4 us
    dot_general x4, matrix products, times_adjoint(): lax.dot_general(left, right, (((1,), (1,)), ((), ())), preferred_element_...  3.89 us
    convert_element_type x1, other arithmetic, on_device(): eff = (beside_all[0, 0].astype(jnp.float32) + beside_all[0, 1].astype(jnp...  1.96 us
    ppermute x1, starting transfers between devices, padded(): after = lax.ppermute(first, axis, down)  1.92 us
  transfers between devices with their start and end apart: 3, of which 3 were waited for; matrix products, arithmetic and copies ran while one was open for 9% of the time, Pallas kernels for 0%

commit v1 on v0

v1 whole, which is shorter than its diff:
```python
import functools

import jax
import jax.numpy as jnp
from jax import lax
from jax.experimental import pallas as pl
from jax.experimental.pallas import tpu as pltpu
from jax.sharding import PartitionSpec as P

CAP = 4
LANES = 128
MESH = pl.DeviceIdType.MESH
F32 = jnp.float32
BF16 = jnp.bfloat16


def iota(shape, dim):
    return lax.broadcasted_iota(jnp.int32, shape, dim)


def repeat(first, last, body):
    if last - first <= 16:
        for k in range(first, last):
            body(k)
    else:
        @pl.loop(first, last)
        def _(k):
            body(k)


def column_of(row, length):
    spread = jnp.broadcast_to(row, (length, length))
    eye = iota((length, length), 0) == iota((length, length), 1)
    return jnp.sum(jnp.where(eye, spread, 0.0), axis=1, keepdims=True)


def dot(left, right):
    return jnp.dot(left, right, preferred_element_type=F32)


def dot_t(left, right):
    return lax.dot_general(left, right, (((1,), (1,)), ((), ())), preferred_element_type=F32)


def kernel(
    count,
    slabs,
    green,
    sigma,
    tiles,
    owner,
    order,
    out,
    g_v,
    s_v,
    tiles_v,
    owner_v,
    order_v,
    inverse,
    a_own,
    a_in,
    q_out,
    q_in,
    p_sum,
    d_out,
    d_in,
    l_out,
    l_in,
    lags,
    load_sem,
    slab_send,
    slab_recv,
    d_send,
    d_recv,
    l_send,
    l_recv,
):
    block = g_v.shape[-1]
    listed = tiles_v.shape[-1]
    rows = 2 * CAP
    me = lax.axis_index("energy")
    slab = lax.axis_index("slab")
    parity = lax.rem(slab, 2)
    near = slab + 1 - 2 * parity
    far = slab - 1 + 2 * parity
    has_far = jnp.logical_and(far >= 0, far < slabs)

    loads = [
        pltpu.make_async_copy(tiles, tiles_v, load_sem.at[0]),
        pltpu.make_async_copy(owner, owner_v, load_sem.at[1]),
        pltpu.make_async_copy(order, order_v, load_sem.at[2]),
        pltpu.make_async_copy(green.at[0, 0], g_v, load_sem.at[3]),
        pltpu.make_async_copy(sigma.at[0, 0], s_v, load_sem.at[4]),
    ]
    for load in loads:
        load.start()

    barrier = pltpu.get_barrier_semaphore()

    def greet(k):
        pl.semaphore_signal(
            barrier, inc=1, device_id={"energy": lax.rem(me + k, count)}, device_id_type=MESH
        )

    repeat(1, count, greet)
    pl.semaphore_signal(barrier, inc=1, device_id={"slab": near}, device_id_type=MESH)

    @pl.when(has_far)
    def _():
        pl.semaphore_signal(barrier, inc=1, device_id={"slab": far}, device_id_type=MESH)

    loads[0].wait()
    tile_col = column_of(tiles_v[...].astype(F32), listed)
    onehot = (iota((listed, block), 1).astype(F32) == tile_col).astype(BF16)
    loads[1].wait()
    own_row = owner_v[...].astype(F32)
    own_col = column_of(own_row, listed)
    earlier = (own_col == own_row) & (iota((listed, listed), 1) < iota((listed, listed), 0))
    rank_col = jnp.sum(jnp.where(earlier, 1.0, 0.0), axis=1, keepdims=True)
    slot_col = own_col * CAP + rank_col
    wide = (listed, 2 * listed)
    spread = iota(wide, 0) == lax.rem(iota(wide, 1), listed)
    slot_row = jnp.sum(jnp.where(spread, slot_col, 0.0), axis=0, keepdims=True)
    full = (count * rows, 2 * listed)
    line = iota(full, 0)
    plane = lax.rem(line, rows) // CAP
    slot = (line // rows) * CAP + lax.rem(line, CAP)
    selector = (
        (slot.astype(F32) == slot_row) & (plane == iota(full, 1) // listed)
    ).astype(BF16)

    loads[3].wait()
    row_re = dot(onehot, g_v[0])
    row_im = dot(onehot, g_v[1])
    a_own[0:listed, :] = row_re.astype(BF16)
    a_own[listed : 2 * listed, :] = row_im.astype(BF16)
    d_re = row_re - dot_t(onehot, g_v[0])
    d_im = row_im + dot_t(onehot, g_v[1])
    d_all = jnp.concatenate([d_re, d_im], axis=0).astype(BF16)
    d_out[...] = dot(selector, d_all).astype(BF16).reshape(count, rows, block)

    pl.semaphore_wait(barrier, count + has_far.astype(jnp.int32))

    def to_slab(src, dst, k, target):
        return pltpu.make_async_remote_copy(
            src_ref=src,
            dst_ref=dst,
            send_sem=slab_send.at[k],
            recv_sem=slab_recv.at[k],
            device_id={"slab": target},
            device_id_type=MESH,
        )

    a_far = to_slab(a_own, a_in.at[1], 1, far)
    a_near = to_slab(a_own, a_in.at[0], 0, near)
    q_far = to_slab(q_out.at[1], q_in.at[1], 3, far)
    q_near = to_slab(q_out.at[0], q_in.at[0], 2, near)

    def to_peer(src, dst, send, recv, k):
        peer = lax.rem(me + k, count)
        return pltpu.make_async_remote_copy(
            src_ref=src.at[peer],
            dst_ref=dst.at[me],
            send_sem=send.at[k],
            recv_sem=recv.at[k],
            device_id={"energy": peer},
            device_id_type=MESH,
        )

    @pl.when(has_far)
    def _():
        a_far.start()

    a_near.start()
    repeat(1, count, lambda k: to_peer(d_out, d_in, d_send, d_recv, k).start())
    d_in[me] = d_out[me]

    loads[2].wait()

    def invert(target):
        def step(k, total):
            return jnp.where(order_v[k] == target, k, total)

        inverse[target] = lax.fori_loop(0, count, step, jnp.int32(0), unroll=count <= 16)

    repeat(0, count, invert)

    def times_sigma(a):
        with_re = dot(a, s_v[0])
        with_im = dot(a, s_v[1])
        return (
            with_re[:listed] - with_im[listed:],
            with_im[:listed] + with_re[listed:],
        )

    loads[4].wait()
    own_re, own_im = times_sigma(a_own[...])
    p_sum[0:listed, :] = own_re
    p_sum[listed : 2 * listed, :] = own_im

    def answer(k):
        part_re, part_im = times_sigma(a_in[k])
        q_out[k, 0:listed, :] = part_re.astype(BF16)
        q_out[k, listed : 2 * listed, :] = part_im.astype(BF16)

    a_near.wait_recv()
    answer(0)
    q_near.start()

    @pl.when(has_far)
    def _():
        a_far.wait_recv()
        answer(1)
        q_far.start()

    q_near.wait_recv()
    p_sum[...] += q_in[0].astype(F32)

    @pl.when(has_far)
    def _():
        q_far.wait_recv()
        p_sum[...] += q_in[1].astype(F32)

    p_all = p_sum[...].astype(BF16)
    with_re = dot_t(p_all, g_v[0])
    with_im = dot_t(p_all, g_v[1])
    l_re = with_re[:listed] + with_im[listed:]
    l_im = with_re[listed:] - with_im[:listed]
    l_all = jnp.concatenate([l_re, l_im], axis=0).astype(BF16)
    l_out[...] = dot(selector, l_all).astype(BF16).reshape(count, rows, block)
    repeat(1, count, lambda k: to_peer(l_out, l_in, l_send, l_recv, k).start())
    l_in[me] = l_out[me]

    def arrived(k):
        to_peer(d_out, d_in, d_send, d_recv, k).wait()
        to_peer(l_out, l_in, l_send, l_recv, k).wait()

    repeat(1, count, arrived)

    def lesser_at(point):
        return l_in[inverse[point]].astype(F32)

    def greater_at(point):
        source = inverse[point]
        return l_in[source].astype(F32) + d_in[source].astype(F32)

    upper = iota((rows, block), 0) < CAP

    def finish(straight, crossed):
        return jnp.where(
            upper,
            straight + pltpu.roll(straight, CAP, 0),
            crossed - pltpu.roll(crossed, CAP, 0),
        ) * (1.0 / count)

    def keep(value, where):
        for chunk in range(block // LANES):
            lags[chunk, where, :] = value[:, chunk * LANES : (chunk + 1) * LANES]

    if count <= 8:
        lesser = [lesser_at(e) for e in range(count)]
        greater = [greater_at(e) for e in range(count)]
        swapped = [pltpu.roll(value, CAP, 0) for value in greater]
        for lag in range(count):
            pairs = range(count - lag)
            straight = sum(lesser[e + lag] * greater[e] for e in pairs)
            crossed = sum(lesser[e + lag] * swapped[e] for e in pairs)
            keep(finish(straight, crossed), pl.ds(lag * rows, rows))
    else:
        @pl.loop(0, count)
        def _(lag):
            def step(e, sums):
                left = lesser_at(e + lag)
                right = greater_at(e)
                return (sums[0] + left * right, sums[1] + left * pltpu.roll(right, CAP, 0))

            zero = jnp.zeros((rows, block), F32)
            straight, crossed = lax.fori_loop(0, count - lag, step, (zero, zero))
            keep(finish(straight, crossed), pl.ds(pl.multiple_of(lag * rows, rows), rows))

    for part in range(2):
        for slot_index in range(CAP):
            for chunk in range(block // LANES):
                out[slot_index, part, :, chunk * LANES : (chunk + 1) * LANES] = lags[
                    chunk, pl.ds(part * CAP + slot_index, count, stride=rows), :
                ].astype(BF16)

    a_near.wait_send()
    q_near.wait_send()

    @pl.when(has_far)
    def _():
        a_far.wait_send()
        q_far.wait_send()


def on_device(green, sigma, tiles, owner, energy_order):
    block = green.shape[-1]
    listed = tiles.shape[1]
    count = lax.axis_size("energy")
    slabs = lax.axis_size("slab")
    rows = 2 * CAP
    anywhere = pl.BlockSpec(memory_space=pl.ANY)
    result = pl.pallas_call(
        functools.partial(kernel, count, slabs),
        out_shape=jax.ShapeDtypeStruct((CAP, 2, count, block), BF16),
        in_specs=[anywhere] * 5,
        out_specs=pl.BlockSpec(memory_space=pltpu.VMEM),
        scratch_shapes=[
            pltpu.VMEM((2, block, block), BF16),
            pltpu.VMEM((2, block, block), BF16),
            pltpu.VMEM((1, listed), jnp.int32),
            pltpu.VMEM((1, listed), jnp.int32),
            pltpu.SMEM((count,), jnp.int32),
            pltpu.SMEM((count,), jnp.int32),
            pltpu.VMEM((2 * listed, block), BF16),
            pltpu.VMEM((2, 2 * listed, block), BF16),
            pltpu.VMEM((2, 2 * listed, block), BF16),
            pltpu.VMEM((2, 2 * listed, block), BF16),
            pltpu.VMEM((2 * listed, block), F32),
            pltpu.VMEM((count, rows, block), BF16),
            pltpu.VMEM((count, rows, block), BF16),
            pltpu.VMEM((count, rows, block), BF16),
            pltpu.VMEM((count, rows, block), BF16),
            pltpu.VMEM((block // LANES, count * rows, LANES), F32),
            pltpu.SemaphoreType.DMA((5,)),
            pltpu.SemaphoreType.DMA((4,)),
            pltpu.SemaphoreType.DMA((4,)),
            pltpu.SemaphoreType.DMA((count,)),
            pltpu.SemaphoreType.DMA((count,)),
            pltpu.SemaphoreType.DMA((count,)),
            pltpu.SemaphoreType.DMA((count,)),
        ],
        compiler_params=pltpu.CompilerParams(collective_id=0, has_side_effects=True),
    )(green, sigma, tiles, owner, energy_order)
    return result.reshape(1, CAP, 2, count, 1, block)


def solution(mesh):
    placed = (
        P("energy", "slab", None, None, None),
        P("energy", "slab", None, None, None),
        P("slab", None),
        P("slab", None),
        P(),
    )
    return jax.shard_map(
        on_device,
        mesh=mesh,
        in_specs=placed,
        out_specs=P("slab", "energy", None, None, None, None),
        check_vma=False,
    )
```

time: 49.1 us -> 17.1 us (0.35)
  waiting for transfers between devices: 16 us -> 0 us
  Pallas kernels: 0 us -> 15.3 us
  starting transfers between devices: 12 us -> 0 us
  local copies, waits for them, and re-layouts: 10.2 us -> 1.47 us
  matrix products: 6.63 us -> 0 us
  other arithmetic: 3.7 us -> 0 us
    pallas_call x0 -> x1, Pallas kernels: none -> 15.3 us  [on_device(): pl.pallas_call(functools.partial(kernel, count, slabs), out_shape=jax.Sha...]
    ppermute x2 -> x0, waiting for transfers between devices: 10 us -> none  [the longest x1 5.6 us: padded(): before = lax.ppermute(last, axis, up)]
    dot_general x11 -> x0, matrix products: 6.63 us -> none  [the longest x4 3.89 us: times_adjoint(): lax.dot_general(left, right, (((1,), (1,)), ((), ())), preferred_element_...]
    ppermute x2 -> x0, starting transfers between devices: 6.41 us -> none  [the longest x1 4.49 us: padded(): before = lax.ppermute(last, axis, up)]
    all_to_all x1 -> x0, waiting for transfers between devices: 6.01 us -> none  [on_device(): lax.all_to_all(outgoing, 'energy', split_axis=0, concat_axis=0, tiled=True)]
    gather x6 -> x0, local copies, waits for them, and re-layouts: 6 us -> none  [the longest x1 1.83 us: on_device(): l_im = full_im[row_index]]
    all_to_all x1 -> x0, starting transfers between devices: 5.56 us -> none  [on_device(): lax.all_to_all(outgoing, 'energy', split_axis=0, concat_axis=0, tiled=True)]
    squeeze x5 -> x0, local copies, waits for them, and re-layouts: 2.4 us -> none  [the longest x3 1.7 us: on_device(): g_re, g_im = (green[0, 0, 0], green[0, 0, 1])]
  transfers between devices with their start and end apart: 3 -> 0, of which waited for: 3 -> 0; matrix products, arithmetic and copies ran while one was open for 9% -> 0% of each run, Pallas kernels for 0% -> 0%
where the time goes in v1:
time: 17.1 us; the launch traced here: 16.8 us
  Pallas kernels  15.3 us (89%)
  local copies, waits for them, and re-layouts  1.47 us (9%)
    pallas_call x1, Pallas kernels, on_device(): pl.pallas_call(functools.partial(kernel, count, slabs), out_shape=jax.Sha...  15.3 us
    unnamed x1, local copies, waits for them, and re-layouts  1.47 us

profile of v1, /device:TPU:1, one launch (start us, length us, event | category | flops | bytes accessed | tf_op | source)
XLA Modules:
  0.0 16.8 jit_solution(6810782499792513208)
XLA Ops:
  0.0 15.3 %shard_map.55 = bf16[4,2,8,512]{3,2,1,0:T(8,128)(2,1)} custom-call(bf16[1,1,2,512,512]{4,3,2,1,0:T(8,128)(2,1)} %green.1, bf16[1,1,2,512,512]{4,3,2,1,0:T(8,128)(2,1)} %sigma.1, s32[1,16]{1,0:T(1,128)} %tiles.1, s32[1,16]{1,0:T(1,128)} %owner.1, s32[8]{0:T(128)} %order.1), custom_call_target="tpu_custom_call" | custom-call | tf_op jit(solution)/shard_map/pallas_call | solution.py:304
  15.4 1.5 %copy.8 = bf16[1,4,2,8,1,512]{5,3,4,2,1,0:T(8,128)(2,1)} copy(bf16[1,4,2,8,1,512]{5,3,4,2,1,0:T(8,128)(2,1)} %bitcast.3) | data formatting | bytes 131072

commit v2 on v1

--- a/solution.py
+++ b/solution.py
@@ -303,7 +303,7 @@
     anywhere = pl.BlockSpec(memory_space=pl.ANY)
     result = pl.pallas_call(
         functools.partial(kernel, count, slabs),
-        out_shape=jax.ShapeDtypeStruct((CAP, 2, count, block), BF16),
+        out_shape=pltpu.VMEM((CAP, 2, count, block), BF16),
         in_specs=[anywhere] * 5,
         out_specs=pl.BlockSpec(memory_space=pltpu.VMEM),
         scratch_shapes=[

time: 17.1 us -> 15.6 us (0.912)
  local copies, waits for them, and re-layouts: 1.47 us -> 0.63 us
  Pallas kernels: 15.3 us -> 14.7 us
    unnamed x1, local copies, waits for them, and re-layouts: 1.47 us -> 0.63 us
    pallas_call x1, Pallas kernels: 15.3 us -> 14.7 us  [on_device(): pl.pallas_call(functools.partial(kernel, count, slabs), out_shape=pltpu.V...]
where the time goes in v2:
time: 15.6 us; the launch traced here: 15.4 us
  Pallas kernels  14.7 us (94%)
  local copies, waits for them, and re-layouts  0.63 us (4%)
    pallas_call x1, Pallas kernels, on_device(): pl.pallas_call(functools.partial(kernel, count, slabs), out_shape=pltpu.V...  14.7 us
    unnamed x1, local copies, waits for them, and re-layouts  0.63 us

profile of v2, /device:TPU:1, one launch (start us, length us, event | category | flops | bytes accessed | tf_op | source)
XLA Modules:
  0.0 15.4 jit_solution(12148398643636295739)
XLA Ops:
  0.0 14.7 %shard_map.55 = bf16[4,2,8,512]{3,2,1,0:T(8,128)(2,1)S(1)} custom-call(bf16[1,1,2,512,512]{4,3,2,1,0:T(8,128)(2,1)} %green.1, bf16[1,1,2,512,512]{4,3,2,1,0:T(8,128)(2,1)} %sigma.1, s32[1,16]{1,0:T(1,128)} %tiles.1, s32[1,16]{1,0:T(1,128)} %owner.1, s32[8]{0:T(128)} %order.1), custom_call_target="tpu_custom_call" | custom-call | tf_op jit(solution)/shard_map/pallas_call | solution.py:304
  14.7 0.6 %copy.8 = bf16[1,4,2,8,1,512]{5,3,4,2,1,0:T(8,128)(2,1)} copy(bf16[1,4,2,8,1,512]{5,3,4,2,1,0:T(8,128)(2,1)S(1)} %bitcast.3) | data formatting | bytes 131072

commit v3 on v2

--- a/solution.py
+++ b/solution.py
@@ -26,6 +26,11 @@
         @pl.loop(first, last)
         def _(k):
             body(k)
+
+
+def bits_of(count):
+    assert count & (count - 1) == 0 and count > 1
+    return [1 << k for k in range(count.bit_length() - 1)]
 
 
 def column_of(row, length):
@@ -74,6 +79,7 @@
     d_recv,
     l_send,
     l_recv,
+    known,
 ):
     block = g_v.shape[-1]
     listed = tiles_v.shape[-1]
@@ -97,12 +103,11 @@
 
     barrier = pltpu.get_barrier_semaphore()
 
-    def greet(k):
+    partners = [me + bit - 2 * bit * lax.rem(me // bit, 2) for bit in bits_of(count)]
+    for partner in partners:
         pl.semaphore_signal(
-            barrier, inc=1, device_id={"energy": lax.rem(me + k, count)}, device_id_type=MESH
+            barrier, inc=1, device_id={"energy": partner}, device_id_type=MESH
         )
-
-    repeat(1, count, greet)
     pl.semaphore_signal(barrier, inc=1, device_id={"slab": near}, device_id_type=MESH)
 
     @pl.when(has_far)
@@ -139,7 +144,7 @@
     d_all = jnp.concatenate([d_re, d_im], axis=0).astype(BF16)
     d_out[...] = dot(selector, d_all).astype(BF16).reshape(count, rows, block)
 
-    pl.semaphore_wait(barrier, count + has_far.astype(jnp.int32))
+    pl.semaphore_wait(barrier, len(partners) + 1 + has_far.astype(jnp.int32))
 
     def to_slab(src, dst, k, target):
         return pltpu.make_async_remote_copy(
@@ -172,8 +177,21 @@
         a_far.start()
 
     a_near.start()
-    repeat(1, count, lambda k: to_peer(d_out, d_in, d_send, d_recv, k).start())
     d_in[me] = d_out[me]
+
+    rounds = len(partners) - 1
+
+    def tell(k):
+        if k < rounds:
+            pl.semaphore_signal(
+                known.at[k], inc=1, device_id={"energy": partners[k]}, device_id_type=MESH
+            )
+
+    def hear(k):
+        if k < rounds:
+            pl.semaphore_wait(known.at[k], 1)
+
+    tell(0)
 
     loads[2].wait()
 
@@ -197,6 +215,8 @@
     own_re, own_im = times_sigma(a_own[...])
     p_sum[0:listed, :] = own_re
     p_sum[listed : 2 * listed, :] = own_im
+    hear(0)
+    tell(1)
 
     def answer(k):
         part_re, part_im = times_sigma(a_in[k])
@@ -212,6 +232,12 @@
         a_far.wait_recv()
         answer(1)
         q_far.start()
+
+    hear(1)
+    for k in range(2, rounds):
+        tell(k)
+        hear(k)
+    repeat(1, count, lambda k: to_peer(d_out, d_in, d_send, d_recv, k).start())
 
     q_near.wait_recv()
     p_sum[...] += q_in[0].astype(F32)
@@ -330,6 +356,7 @@
             pltpu.SemaphoreType.DMA((count,)),
             pltpu.SemaphoreType.DMA((count,)),
             pltpu.SemaphoreType.DMA((count,)),
+            pltpu.SemaphoreType.REGULAR((len(bits_of(count)),)),
         ],
         compiler_params=pltpu.CompilerParams(collective_id=0, has_side_effects=True),
     )(green, sigma, tiles, owner, energy_order)

time: 15.6 us -> 15.5 us (level)
  no operation moved by 1% of the time
where the time goes in v3:
time: 15.5 us; the launch traced here: 15.4 us
  Pallas kernels  14.8 us (95%)
  local copies, waits for them, and re-layouts  0.63 us (4%)
    pallas_call x1, Pallas kernels, on_device(): pl.pallas_call(functools.partial(kernel, count, slabs), out_shape=pltpu.V...  14.8 us
    unnamed x1, local copies, waits for them, and re-layouts  0.63 us

profile of v3, /device:TPU:1, one launch (start us, length us, event | category | flops | bytes accessed | tf_op | source)
XLA Modules:
  0.0 15.4 jit_solution(1667440124604577043)
XLA Ops:
  0.0 14.8 %shard_map.55 = bf16[4,2,8,512]{3,2,1,0:T(8,128)(2,1)S(1)} custom-call(bf16[1,1,2,512,512]{4,3,2,1,0:T(8,128)(2,1)} %green.1, bf16[1,1,2,512,512]{4,3,2,1,0:T(8,128)(2,1)} %sigma.1, s32[1,16]{1,0:T(1,128)} %tiles.1, s32[1,16]{1,0:T(1,128)} %owner.1, s32[8]{0:T(128)} %order.1), custom_call_target="tpu_custom_call" | custom-call | tf_op jit(solution)/shard_map/pallas_call | solution.py:330
  14.8 0.6 %copy.8 = bf16[1,4,2,8,1,512]{5,3,4,2,1,0:T(8,128)(2,1)} copy(bf16[1,4,2,8,1,512]{5,3,4,2,1,0:T(8,128)(2,1)S(1)} %bitcast.3) | data formatting | bytes 131072
